TPU v7x, 256 devices: a whole 4x4x8 slice. The times are simulated.
256 devices in a mesh: dp: 4 (over y), graph: 64 (over z, x, core).
Axes of the slice: x: 4, y: 4, z: 8, core: 2. Of those that a mesh axis runs over, the one named last changes fastest.
Arguments:
- edge_state: bfloat16 [4, 131072, 512], P('dp', 'graph'), may hold values from -6 to 6
- cotangent: bfloat16 [4, 131072, 512], P('dp', 'graph'), may hold values from -6 to 6
- edge_count: int32 [4, 64], P('dp', 'graph'), may hold values from 1024 to 2048, as said below
- triplet_basis: bfloat16 [4, 16, 524288], P('dp', None, 'graph'), may hold values from -6 to 6
- triplet_in: int32 [4, 524288], P('dp', 'graph'), may hold values from 0 to 2047, as said below
- triplet_out: int32 [4, 524288], P('dp', 'graph'), may hold values from 0 to 2047, as said below
- down_weight: bfloat16 [512, 64], replicated, may hold values from -0.25 to 0.25
- basis_weight: bfloat16 [16, 64], replicated, may hold values from -1.5 to 1.5
- bilinear_weight: bfloat16 [64, 64], replicated, may hold values from -0.75 to 0.75
- up_weight: bfloat16 [64, 512], replicated, may hold values from -0.75 to 0.75
- first_weight: bfloat16 [512, 512], replicated, may hold values from -0.25 to 0.25
- second_weight: bfloat16 [512, 512], replicated, may hold values from -0.25 to 0.25
Outputs:
- edge_grad: bfloat16 [4, 131072, 512], P('dp', 'graph')
- down_grad: float32 [512, 64], replicated
- basis_grad: float32 [16, 64], replicated
- bilinear_grad: float32 [64, 64], replicated
- up_grad: float32 [64, 512], replicated
- first_grad: float32 [512, 512], replicated
- second_grad: float32 [512, 512], replicated
Inputs may be any that keep to these rules, and one draw needn't show every extreme that they name: `edge_count`: every entry is a multiple of 128; in every batch some shard holds all 2048 slots live. Slot s * 8192 + j * 128 + k (s and j below 64, k below 128) holds a triplet of shard s whose in-edge is row triplet_in of shard j, a live row: below edge_count[b, j]. Slot s * 8192 + t holds a triplet whose out-edge is row triplet_out of shard s, a live row: below edge_count[b, s].
All inputs are finite; a program needn't handle non-finite values.
Results may differ from a plain program's by a relative error of at most 0.0096.
Values may be sent and summed in bfloat16 or wider, within the bound.
A program may use at most 128 MiB of HBM per device.

v0:
```python
import math
import jax
import jax.numpy as jnp
from jax import lax
from jax.sharding import PartitionSpec as P

HALF = 0.7071067811865476


def silu_slope(argument):
    logistic = jax.nn.sigmoid(argument)
    return logistic * (1.0 + argument * (1.0 - logistic))


def contract(left, right, left_dim, right_dim):
    return lax.dot_general(
        left, right, (((left_dim,), (right_dim,)), ((), ())), preferred_element_type=jnp.float32
    )


def local(
    edge_state,
    cotangent,
    edge_count,
    triplet_basis,
    triplet_in,
    triplet_out,
    down_weight,
    basis_weight,
    bilinear_weight,
    up_weight,
    first_weight,
    second_weight,
):
    edge_rows = edge_state[0]
    row_count = edge_rows.shape[0]
    shards = lax.axis_size("graph")
    narrow = down_weight.shape[1]
    in_local = triplet_in[0]
    out_local = triplet_out[0]
    tri_rows = in_local.shape[0]
    slot_count = tri_rows // shards
    live_mask = (jnp.arange(row_count, dtype=jnp.int32) < edge_count[0, 0]).astype(jnp.float32)
    wanted = lax.all_to_all(
        in_local.reshape(shards, slot_count), "graph", split_axis=0, concat_axis=0, tiled=True
    ).reshape(tri_rows)
    pre_down = contract(down_weight, edge_rows, 0, 1)
    down_rows = jax.nn.silu(pre_down).astype(jnp.bfloat16)
    tri_coef = contract(basis_weight, triplet_basis[0], 0, 0)
    served = jnp.take(down_rows, wanted, axis=1).reshape(narrow, shards, slot_count)
    fetched = lax.all_to_all(served, "graph", split_axis=1, concat_axis=1, tiled=True).reshape(
        narrow, tri_rows
    )
    message = tri_coef * fetched.astype(jnp.float32)
    gathered = (
        jnp.zeros((narrow, row_count), jnp.float32)
        .at[:, out_local]
        .add(message)
        .astype(jnp.bfloat16)
    )
    mixed_rows = contract(bilinear_weight, gathered, 0, 0).astype(jnp.bfloat16)
    pre_up = contract(mixed_rows, up_weight, 0, 0)
    summed = edge_rows.astype(jnp.float32) + jax.nn.silu(pre_up)
    summed_half = summed.astype(jnp.bfloat16)
    pre_first = jnp.dot(summed_half, first_weight, preferred_element_type=jnp.float32)
    first_rows = jax.nn.silu(pre_first).astype(jnp.bfloat16)
    pre_second = jnp.dot(first_rows, second_weight, preferred_element_type=jnp.float32)
    back_top = cotangent[0].astype(jnp.float32) * live_mask[:, None] * HALF
    back_second = (back_top * silu_slope(pre_second)).astype(jnp.bfloat16)
    back_first = (contract(back_second, second_weight, 1, 1) * silu_slope(pre_first)).astype(
        jnp.bfloat16
    )
    first_grad = contract(summed_half, back_first, 0, 0)
    second_grad = contract(first_rows, back_second, 0, 0)
    back_summed = back_top + contract(back_first, first_weight, 1, 1)
    back_up = (back_summed * silu_slope(pre_up)).astype(jnp.bfloat16)
    back_mixed = contract(up_weight, back_up, 1, 1).astype(jnp.bfloat16)
    back_gathered = contract(bilinear_weight, back_mixed, 1, 0)
    back_message = jnp.take(back_gathered, out_local, axis=1)
    back_coef = (back_message * fetched.astype(jnp.float32)).astype(jnp.bfloat16)
    back_fetched = back_message * tri_coef
    returned = (
        lax.all_to_all(
            back_fetched.reshape(narrow, shards, slot_count).astype(jnp.bfloat16),
            "graph",
            split_axis=1,
            concat_axis=1,
            tiled=True,
        )
        .astype(jnp.float32)
        .reshape(narrow, tri_rows)
    )
    back_down = jnp.zeros((narrow, row_count), jnp.float32).at[:, wanted].add(returned)
    up_grad = contract(mixed_rows, back_up, 1, 0)
    bilinear_grad = contract(gathered, back_mixed, 1, 1)
    basis_grad = contract(triplet_basis[0], back_coef, 1, 1)
    back_pre = (back_down * silu_slope(pre_down)).astype(jnp.bfloat16)
    down_grad = contract(edge_rows, back_pre, 0, 1)
    edge_grad = (back_summed + contract(back_pre, down_weight, 0, 1)).astype(jnp.bfloat16)
    down_grad, basis_grad, bilinear_grad, up_grad, first_grad, second_grad = lax.psum(
        (down_grad, basis_grad, bilinear_grad, up_grad, first_grad, second_grad), ("dp", "graph")
    )
    grad_scale = 1.0 / math.sqrt(lax.axis_size("dp") * shards * row_count)
    return (
        edge_grad[None],
        down_grad * grad_scale,
        basis_grad * grad_scale,
        bilinear_grad * grad_scale,
        up_grad * grad_scale,
        first_grad * grad_scale,
        second_grad * grad_scale,
    )


def solution(mesh):
    in_specs = (
        P("dp", "graph", None),
        P("dp", "graph", None),
        P("dp", "graph"),
        P("dp", None, "graph"),
        P("dp", "graph"),
        P("dp", "graph"),
        P(),
        P(),
        P(),
        P(),
        P(),
        P(),
    )
    out_specs = (P("dp", "graph", None), P(), P(), P(), P(), P(), P())
    return jax.shard_map(local, mesh=mesh, in_specs=in_specs, out_specs=out_specs, check_vma=False)
```

profile of v0, /device:TPU:2, one launch (start us, length us, event | category | flops | bytes accessed | tf_op | source)
XLA Modules:
  0.0 558.6 jit_solution(4663164017009512426)
XLA Ops:
  7.2 12.2 %all-to-all-start = ((s32[64,1,128]{2,1,0:T(1,128)}), s32[64,1,128]{2,1,0:T(1,128)S(1)}, u32[]{:S(2)}, u32[]{:S(2)}) async-start(s32[64,1,128]{2,1,0:T(1,128)} %bitcast.127), calls=%async_computation | async-start | bytes 65536 | tf_op jit(solution)/shard_map/all_to_all | solution.py:44
  20.8 3.2 multiply_convert_fusion.4
  24.3 3.6 all-to-all-done
  28.0 24.0 %gather_fusion = bf16[8192,64]{1,0:T(8,128)(2,1)S(1)} fusion(bf16[64,2048]{0,1:T(8,128)(2,1)S(1)} %copy.35, s32[8192]{0:T(1024)S(1)} %broadcast_clamp_fusion.1), kind=kCustom, calls=%fused_computation | custom fusion | bytes 2129920 | tf_op jit(solution)/shard_map/jit(_take)/gather | solution.py:50
  56.0 6.9 %all-to-all-start.1 = ((bf16[64,64,128]{2,0,1:T(8,128)(2,1)}), bf16[64,64,128]{2,0,1:T(8,128)(2,1)}, u32[]{:S(2)}, u32[]{:S(2)}) async-start(bf16[64,64,128]{2,0,1:T(8,128)(2,1)} %broadcast_select_fusion), calls=%async_computation.1 | async-start | bytes 2097152 | tf_op jit(solution)/shard_map/all_to_all | solution.py:51
  63.4 28.1 %all-to-all-done.1 = bf16[64,64,128]{2,0,1:T(8,128)(2,1)} async-done(((bf16[64,64,128]{2,0,1:T(8,128)(2,1)}), bf16[64,64,128]{2,0,1:T(8,128)(2,1)}, u32[]{:S(2)}, u32[]{:S(2)}) %all-to-all-start.1) | async-done | bytes 1048608 | tf_op jit(solution)/shard_map/all_to_all | solution.py:51
  91.5 2.7 fusion.6
  94.3 3.8 copy.38
  98.1 45.3 %scatter_custom_fusion = f32[64,2048]{0,1:T(8,128)} fusion(s32[8192]{0:T(1024)S(1)} %bitcast.126, f32[8192,64]{1,0:T(8,128)} %copy.38, f32[]{:T(128)} %constant.18.clone.1), kind=kCustom, calls=%fused_computation.50 | custom fusion | flops 524288 | bytes 524800 | tf_op jit(solution)/shard_map/scatter-add | solution.py:58
  144.9 2.9 add_convert_fusion.1
  155.3 4.0 multiply_convert_fusion
  163.6 27.9 %gather_fusion.1 = f32[8192,64]{1,0:T(8,128)} fusion(f32[64,2048]{0,1:T(8,128)S(1)} %copy.39, s32[8192]{0:T(1024)S(1)} %broadcast_clamp_fusion), kind=kCustom, calls=%fused_computation.1 | custom fusion | bytes 4227072 | tf_op jit(solution)/shard_map/jit(_take)/gather | solution.py:79
  191.6 3.8 copy.40
  195.3 2.9 copy_bitcast_fusion
  198.2 5.8 %all-to-all-start.2 = ((bf16[64,64,128]{2,0,1:T(8,128)(2,1)}), bf16[64,64,128]{2,0,1:T(8,128)(2,1)S(1)}, u32[]{:S(2)}, u32[]{:S(2)}) async-start(bf16[64,64,128]{2,0,1:T(8,128)(2,1)} %copy_bitcast_fusion), calls=%async_computation.2 | async-start | bytes 2097152 | tf_op jit(solution)/shard_map/all_to_all | solution.py:83
  206.0 4.0 fusion.33
  212.3 20.6 %all-to-all-done.2 = bf16[64,64,128]{2,0,1:T(8,128)(2,1)S(1)} async-done(((bf16[64,64,128]{2,0,1:T(8,128)(2,1)}), bf16[64,64,128]{2,0,1:T(8,128)(2,1)S(1)}, u32[]{:S(2)}, u32[]{:S(2)}) %all-to-all-start.2) | async-done | bytes 1048608 | tf_op jit(solution)/shard_map/all_to_all | solution.py:83
  233.0 2.8 copy.43
  235.8 44.6 %scatter_custom_fusion.1 = f32[64,2048]{0,1:T(8,128)S(1)} fusion(s32[8192]{0:T(1024)S(1)} %bitcast.124, f32[8192,64]{1,0:T(8,128)} %copy.43, f32[]{:T(128)} %constant.18.clone.1), kind=kCustom, calls=%fused_computation.48 | custom fusion | flops 524288 | bytes 524800 | tf_op jit(solution)/shard_map/scatter-add | solution.py:93
  280.9 2.8 fusion.13
  287.1 74.4 %all-reduce = (f32[16,64]{1,0:T(8,128)S(1)}, f32[64,64]{1,0:T(8,128)S(1)}) all-reduce(f32[16,64]{1,0:T(8,128)S(1)} %convolution_bitcast_fusion.1, f32[64,64]{1,0:T(8,128)S(1)} %fusion.27), channel_id=1, replica_groups=mesh['dp'=4,'graph'=64] {'dp','graph'}, use_global_device_ids=true, to_apply=%region_3.4 | all-reduce | flops 5120 | bytes 40960 | tf_op jit(solution)/shard_map/psum | solution.py:100
  362.7 4.3 fusion.4
  367.0 178.4 %all-reduce.4.cloned.1.call-done = (f32[512,64]{0,1:T(8,128)}, f32[64,512]{1,0:T(8,128)}, f32[512,512]{1,0:T(8,128)}, f32[512,512]{1,0:T(8,128)}) async-done(((f32[512,64]{0,1:T(8,128)}, f32[64,512]{1,0:T(8,128)}, f32[512,512]{1,0:T(8,128)}, f32[512,512]{1,0:T(8,128)}), (f32[512,64]{0,1:T(8,128)}, f32[64,512]{1,0:T(8,128)}, f32[512,512]{1,0:T(8,128)}, f32[512,512]{1,0:T(8,128)})) %all-reduce.4.cloned.1.call-update) | async-done | bytes 2359312 | tf_op jit(solution)/shard_map/psum | solution.py:100
  548.6 3.2 broadcast_multiply_fusion
  (78 shorter events, 31.4 us)
Async XLA Ops:
  7.2 140.7 %copy-start = (bf16[512,512]{1,0:T(8,128)(2,1)S(1)}, bf16[512,512]{1,0:T(8,128)(2,1)}, u32[]{:S(2)}) copy-start(bf16[512,512]{1,0:T(8,128)(2,1)} %param.22) | copy-start | bytes 1572868
  7.2 20.7 %all-to-all-start = ((s32[64,1,128]{2,1,0:T(1,128)}), s32[64,1,128]{2,1,0:T(1,128)S(1)}, u32[]{:S(2)}, u32[]{:S(2)}) async-start(s32[64,1,128]{2,1,0:T(1,128)} %bitcast.127), calls=%async_computation | async-start | bytes 65536 | tf_op jit(solution)/shard_map/all_to_all | solution.py:44
  53.6 9.2 %copy-start.8 = (s32[1,8192]{1,0:T(1,128)S(1)}, s32[1,8192]{1,0:T(1,128)}, u32[]{:S(2)}) copy-start(s32[1,8192]{1,0:T(1,128)} %param.17) | copy-start | bytes 98308
  53.6 9.3 %copy-start.9 = (bf16[1,16,8192]{2,1,0:T(8,128)(2,1)S(1)}, bf16[1,16,8192]{2,1,0:T(8,128)(2,1)}, u32[]{:S(2)}) copy-start(bf16[1,16,8192]{2,1,0:T(8,128)(2,1)} %param.15) | copy-start | bytes 786436
  53.6 9.3 %copy-start.13 = (bf16[16,64]{1,0:T(8,128)(2,1)S(1)}, bf16[16,64]{1,0:T(8,128)(2,1)}, u32[]{:S(2)}) copy-start(bf16[16,64]{1,0:T(8,128)(2,1)} %param.19) | copy-start | bytes 6148
  56.0 35.6 %all-to-all-start.1 = ((bf16[64,64,128]{2,0,1:T(8,128)(2,1)}), bf16[64,64,128]{2,0,1:T(8,128)(2,1)}, u32[]{:S(2)}, u32[]{:S(2)}) async-start(bf16[64,64,128]{2,0,1:T(8,128)(2,1)} %broadcast_select_fusion), calls=%async_computation.1 | async-start | bytes 2097152 | tf_op jit(solution)/shard_map/all_to_all | solution.py:51
  94.3 49.1 %copy-start.12 = (bf16[64,64]{1,0:T(8,128)(2,1)S(1)}, bf16[64,64]{1,0:T(8,128)(2,1)}, u32[]{:S(2)}) copy-start(bf16[64,64]{1,0:T(8,128)(2,1)} %param.20) | copy-start | bytes 24580
  98.1 46.9 %copy-start.11 = (bf16[64,512]{1,0:T(8,128)(2,1)S(1)}, bf16[64,512]{1,0:T(8,128)(2,1)}, u32[]{:S(2)}) copy-start(bf16[64,512]{1,0:T(8,128)(2,1)} %param.21) | copy-start | bytes 196612
  147.8 1.9 copy-start.16
  147.8 2.3 copy-start.14
  147.9 2.4 copy-start.15
  149.8 3.1 copy-start.20
  152.9 2.3 copy-start.22
  155.2 4.0 copy-start.18
  198.2 6.1 %copy-start.5 = (bf16[2048,512]{1,0:T(8,128)(2,1)S(1)}, bf16[2048,512]{1,0:T(8,128)(2,1)}, u32[]{:S(2)}) copy-start(bf16[2048,512]{1,0:T(8,128)(2,1)} %copy-done.4) | copy-start | bytes 6291460
  198.2 34.6 %all-to-all-start.2 = ((bf16[64,64,128]{2,0,1:T(8,128)(2,1)}), bf16[64,64,128]{2,0,1:T(8,128)(2,1)S(1)}, u32[]{:S(2)}, u32[]{:S(2)}) async-start(bf16[64,64,128]{2,0,1:T(8,128)(2,1)} %copy_bitcast_fusion), calls=%async_computation.2 | async-start | bytes 2097152 | tf_op jit(solution)/shard_map/all_to_all | solution.py:83
  204.0 341.4 %all-reduce.4.cloned.1.call-start = ((), (), s32[]{:S(2)}) async-start(), calls=%async_computation.3 | async-start | bytes 4718592 | tf_op jit(solution)/shard_map/psum | solution.py:100
  206.0 4.0 copy-start.17
  206.0 4.0 copy-start.19
  235.8 44.9 %copy-start.7 = (f32[64,2048]{1,0:T(8,128)S(1)}, f32[64,2048]{1,0:T(8,128)}, u32[]{:S(2)}) copy-start(f32[64,2048]{1,0:T(8,128)} %get-tuple-element.14) | copy-start | bytes 1572868
  280.9 2.9 copy-start.2
  283.7 1.7 copy-start.3
  285.4 77.3 %copy-start.10 = (bf16[512,64]{0,1:T(8,128)(2,1)S(1)}, bf16[512,64]{0,1:T(8,128)(2,1)}, u32[]{:S(2)}) copy-start(bf16[512,64]{0,1:T(8,128)(2,1)} %param.18) | copy-start | bytes 196612
  548.6 3.2 copy-start.1
  (3 other events, 3.7 us)
Sparse Core Ops, SparseCore 0:
  283.9 261.4 all-reduce.3
where the time goes:
time: 560 us; the launch traced here: 559 us
  waiting for transfers between devices  231 us (41%)
  other arithmetic  107 us (19%)
  blocking collectives  74.4 us (13%)
  local copies, waits for them, and re-layouts  68.5 us (12%)
  matrix products  38.2 us (7%)
  starting transfers between devices  25.1 us (4%)
  between operations  15 us (3%)
    psum x1, waiting for transfers between devices, local(): lax.psum((down_grad, basis_grad, bilinear_grad, up_grad, first_grad, seco...  178 us
    psum x1, blocking collectives, local(): lax.psum((down_grad, basis_grad, bilinear_grad, up_grad, first_grad, seco...  74.4 us
    scatter-add x1, other arithmetic, local(): gathered = jnp.zeros((narrow, row_count), jnp.float32).at[:, out_local].a...  45.3 us
    scatter-add x1, other arithmetic, local(): jnp.zeros((narrow, row_count), jnp.float32).at[:, wanted].add(returned)  44.6 us
    dot_general x15, matrix products, contract(): lax.dot_general(left, right, (((left_dim,), (right_dim,)), ((), ())), pre...  33.7 us
    gather x2, local copies, waits for them, and re-layouts, local(): back_message = jnp.take(back_gathered, out_local, axis=1)  31.7 us
    all_to_all x1, waiting for transfers between devices, local(): lax.all_to_all(served, 'graph', split_axis=1, concat_axis=1, tiled=True)  28.1 us
    gather x2, local copies, waits for them, and re-layouts, local(): jnp.take(down_rows, wanted, axis=1).reshape(narrow, shards, slot_count)  25.6 us
  transfers between devices with their start and end apart: 4, of which 4 were waited for; matrix products, arithmetic and copies ran while one was open for 4% of the time, Pallas kernels for 0%

commit v1 on v0

--- a/solution.py
+++ b/solution.py
@@ -98,7 +98,8 @@
     down_grad = contract(edge_rows, back_pre, 0, 1)
     edge_grad = (back_summed + contract(back_pre, down_weight, 0, 1)).astype(jnp.bfloat16)
     down_grad, basis_grad, bilinear_grad, up_grad, first_grad, second_grad = lax.psum(
-        (down_grad, basis_grad, bilinear_grad, up_grad, first_grad, second_grad), ("dp", "graph")
+        lax.psum((down_grad, basis_grad, bilinear_grad, up_grad, first_grad, second_grad), "dp"),
+        "graph",
     )
     grad_scale = 1.0 / math.sqrt(lax.axis_size("dp") * shards * row_count)
     return (

time: 560 us -> 633 us (1.13)
  blocking collectives: 74.4 us -> 258 us
  waiting for transfers between devices: 231 us -> 117 us
    psum x0 -> x1, blocking collectives: none -> 242 us  [local(): lax.psum(lax.psum((down_grad, basis_grad, bilinear_grad, up_grad, first_g...]
    psum x1, waiting for transfers between devices: 178 us -> 64.8 us  [local(): lax.psum((down_grad, basis_grad, bilinear_grad, up_grad, first_grad, seco...]
    psum x1, blocking collectives: 74.4 us -> 15.4 us  [local(): lax.psum((down_grad, basis_grad, bilinear_grad, up_grad, first_grad, seco...]
  transfers between devices with their start and end apart: 4 -> 5, of which waited for: 4 -> 4; matrix products, arithmetic and copies ran while one was open for 4% -> 3% of each run, Pallas kernels for 0% -> 0%
where the time goes in v1:
time: 633 us; the launch traced here: 628 us
  blocking collectives  258 us (41%)
  waiting for transfers between devices  117 us (18%)
  other arithmetic  107 us (17%)
  local copies, waits for them, and re-layouts  68.3 us (11%)
  matrix products  37.9 us (6%)
  starting transfers between devices  25.1 us (4%)
  between operations  15.1 us (2%)
    psum x1, blocking collectives, local(): lax.psum(lax.psum((down_grad, basis_grad, bilinear_grad, up_grad, first_g...  242 us
    psum x1, waiting for transfers between devices, local(): lax.psum((down_grad, basis_grad, bilinear_grad, up_grad, first_grad, seco...  64.8 us
    scatter-add x1, other arithmetic, local(): gathered = jnp.zeros((narrow, row_count), jnp.float32).at[:, out_local].a...  45.3 us
    scatter-add x1, other arithmetic, local(): jnp.zeros((narrow, row_count), jnp.float32).at[:, wanted].add(returned)  44.6 us
    dot_general x15, matrix products, contract(): lax.dot_general(left, right, (((left_dim,), (right_dim,)), ((), ())), pre...  33.4 us
    gather x2, local copies, waits for them, and re-layouts, local(): back_message = jnp.take(back_gathered, out_local, axis=1)  31.7 us
    all_to_all x1, waiting for transfers between devices, local(): lax.all_to_all(served, 'graph', split_axis=1, concat_axis=1, tiled=True)  28.1 us
    gather x2, local copies, waits for them, and re-layouts, local(): jnp.take(down_rows, wanted, axis=1).reshape(narrow, shards, slot_count)  25.6 us
  transfers between devices with their start and end apart: 5, of which 4 were waited for; matrix products, arithmetic and copies ran while one was open for 3% of the time, Pallas kernels for 0%

profile of v1, /device:TPU:2, one launch (start us, length us, event | category | flops | bytes accessed | tf_op | source)
XLA Modules:
  0.0 627.9 jit_solution(7937937274104300608)
XLA Ops:
  7.2 12.2 %all-to-all-start = ((s32[64,1,128]{2,1,0:T(1,128)}), s32[64,1,128]{2,1,0:T(1,128)S(1)}, u32[]{:S(2)}, u32[]{:S(2)}) async-start(s32[64,1,128]{2,1,0:T(1,128)} %bitcast.127), calls=%async_computation | async-start | bytes 65536 | tf_op jit(solution)/shard_map/all_to_all | solution.py:44
  20.8 3.2 multiply_convert_fusion.4
  24.3 3.6 all-to-all-done
  28.0 24.0 %gather_fusion = bf16[8192,64]{1,0:T(8,128)(2,1)S(1)} fusion(bf16[64,2048]{0,1:T(8,128)(2,1)S(1)} %copy.35, s32[8192]{0:T(1024)S(1)} %broadcast_clamp_fusion.1), kind=kCustom, calls=%fused_computation | custom fusion | bytes 2129920 | tf_op jit(solution)/shard_map/jit(_take)/gather | solution.py:50
  56.0 6.9 %all-to-all-start.1 = ((bf16[64,64,128]{2,0,1:T(8,128)(2,1)}), bf16[64,64,128]{2,0,1:T(8,128)(2,1)}, u32[]{:S(2)}, u32[]{:S(2)}) async-start(bf16[64,64,128]{2,0,1:T(8,128)(2,1)} %broadcast_select_fusion), calls=%async_computation.1 | async-start | bytes 2097152 | tf_op jit(solution)/shard_map/all_to_all | solution.py:51
  63.4 28.1 %all-to-all-done.1 = bf16[64,64,128]{2,0,1:T(8,128)(2,1)} async-done(((bf16[64,64,128]{2,0,1:T(8,128)(2,1)}), bf16[64,64,128]{2,0,1:T(8,128)(2,1)}, u32[]{:S(2)}, u32[]{:S(2)}) %all-to-all-start.1) | async-done | bytes 1048608 | tf_op jit(solution)/shard_map/all_to_all | solution.py:51
  91.5 2.7 fusion.6
  94.3 3.8 copy.38
  98.1 45.3 %scatter_custom_fusion = f32[64,2048]{0,1:T(8,128)} fusion(s32[8192]{0:T(1024)S(1)} %bitcast.126, f32[8192,64]{1,0:T(8,128)} %copy.38, f32[]{:T(128)} %constant.18.clone.1), kind=kCustom, calls=%fused_computation.50 | custom fusion | flops 524288 | bytes 524800 | tf_op jit(solution)/shard_map/scatter-add | solution.py:58
  144.9 2.9 add_convert_fusion.1
  155.3 4.0 multiply_convert_fusion
  163.6 27.9 %gather_fusion.1 = f32[8192,64]{1,0:T(8,128)} fusion(f32[64,2048]{0,1:T(8,128)S(1)} %copy.39, s32[8192]{0:T(1024)S(1)} %broadcast_clamp_fusion), kind=kCustom, calls=%fused_computation.1 | custom fusion | bytes 4227072 | tf_op jit(solution)/shard_map/jit(_take)/gather | solution.py:79
  191.6 3.8 copy.40
  195.3 2.9 copy_bitcast_fusion
  198.2 5.8 all-to-all-start.2
  206.0 4.0 fusion.33
  212.3 20.6 %all-to-all-done.2 = bf16[64,64,128]{2,0,1:T(8,128)(2,1)S(1)} async-done(((bf16[64,64,128]{2,0,1:T(8,128)(2,1)}), bf16[64,64,128]{2,0,1:T(8,128)(2,1)S(1)}, u32[]{:S(2)}, u32[]{:S(2)}) %all-to-all-start.2) | async-done | bytes 1048608 | tf_op jit(solution)/shard_map/all_to_all | solution.py:83
  233.0 2.8 copy.43
  235.8 44.6 %scatter_custom_fusion.1 = f32[64,2048]{0,1:T(8,128)S(1)} fusion(s32[8192]{0:T(1024)S(1)} %bitcast.124, f32[8192,64]{1,0:T(8,128)} %copy.43, f32[]{:T(128)} %constant.18.clone.1), kind=kCustom, calls=%fused_computation.48 | custom fusion | flops 524288 | bytes 524800 | tf_op jit(solution)/shard_map/scatter-add | solution.py:93
  283.8 64.8 %all-reduce.9.cloned.1.call-done = (f32[512,64]{0,1:T(8,128)}, f32[64,512]{1,0:T(8,128)}, f32[512,512]{1,0:T(8,128)}, f32[512,512]{1,0:T(8,128)}) async-done(((f32[512,64]{0,1:T(8,128)}, f32[64,512]{1,0:T(8,128)}, f32[512,512]{1,0:T(8,128)}, f32[512,512]{1,0:T(8,128)}), (f32[512,64]{0,1:T(8,128)}, f32[64,512]{1,0:T(8,128)}, f32[512,512]{1,0:T(8,128)}, f32[512,512]{1,0:T(8,128)})) %all-reduce.9.cloned.1.call-update) | async-done | bytes 2359312 | tf_op jit(solution)/shard_map/psum | solution.py:101
  351.6 15.4 %all-reduce.2 = (f32[16,64]{1,0:T(8,128)S(1)}, f32[64,64]{1,0:T(8,128)S(1)}) all-reduce(f32[16,64]{1,0:T(8,128)S(1)} %convolution_bitcast_fusion.1, f32[64,64]{1,0:T(8,128)S(1)} %fusion.27), channel_id=1, replica_groups=mesh['dp'=4,'graph'=64] {'dp'}, use_global_device_ids=true, to_apply=%region_4.5 | all-reduce | flops 5120 | bytes 40960 | tf_op jit(solution)/shard_map/psum | solution.py:101
  367.0 242.2 %all-reduce = (f32[16,64]{1,0:T(8,128)S(1)}, f32[64,64]{1,0:T(8,128)S(1)}) all-reduce(f32[16,64]{1,0:T(8,128)S(1)} %get-tuple-element.13, f32[64,64]{1,0:T(8,128)S(1)} %get-tuple-element.14), channel_id=1, replica_groups=mesh['dp'=4,'graph'=64] {'graph'}, use_global_device_ids=true, to_apply=%region_5.6 | all-reduce | flops 5120 | bytes 40960 | tf_op jit(solution)/shard_map/psum | solution.py:100
  610.5 4.2 fusion.4
  617.9 3.2 broadcast_multiply_fusion
  (82 shorter events, 33.8 us)
Async XLA Ops:
  7.2 140.7 %copy-start = (bf16[512,512]{1,0:T(8,128)(2,1)S(1)}, bf16[512,512]{1,0:T(8,128)(2,1)}, u32[]{:S(2)}) copy-start(bf16[512,512]{1,0:T(8,128)(2,1)} %param.22) | copy-start | bytes 1572868
  7.2 20.7 %all-to-all-start = ((s32[64,1,128]{2,1,0:T(1,128)}), s32[64,1,128]{2,1,0:T(1,128)S(1)}, u32[]{:S(2)}, u32[]{:S(2)}) async-start(s32[64,1,128]{2,1,0:T(1,128)} %bitcast.127), calls=%async_computation | async-start | bytes 65536 | tf_op jit(solution)/shard_map/all_to_all | solution.py:44
  53.6 9.2 %copy-start.8 = (s32[1,8192]{1,0:T(1,128)S(1)}, s32[1,8192]{1,0:T(1,128)}, u32[]{:S(2)}) copy-start(s32[1,8192]{1,0:T(1,128)} %param.17) | copy-start | bytes 98308
  53.6 9.3 %copy-start.9 = (bf16[1,16,8192]{2,1,0:T(8,128)(2,1)S(1)}, bf16[1,16,8192]{2,1,0:T(8,128)(2,1)}, u32[]{:S(2)}) copy-start(bf16[1,16,8192]{2,1,0:T(8,128)(2,1)} %param.15) | copy-start | bytes 786436
  53.6 9.3 %copy-start.13 = (bf16[16,64]{1,0:T(8,128)(2,1)S(1)}, bf16[16,64]{1,0:T(8,128)(2,1)}, u32[]{:S(2)}) copy-start(bf16[16,64]{1,0:T(8,128)(2,1)} %param.19) | copy-start | bytes 6148
  56.0 35.6 %all-to-all-start.1 = ((bf16[64,64,128]{2,0,1:T(8,128)(2,1)}), bf16[64,64,128]{2,0,1:T(8,128)(2,1)}, u32[]{:S(2)}, u32[]{:S(2)}) async-start(bf16[64,64,128]{2,0,1:T(8,128)(2,1)} %broadcast_select_fusion), calls=%async_computation.1 | async-start | bytes 2097152 | tf_op jit(solution)/shard_map/all_to_all | solution.py:51
  94.3 49.1 %copy-start.12 = (bf16[64,64]{1,0:T(8,128)(2,1)S(1)}, bf16[64,64]{1,0:T(8,128)(2,1)}, u32[]{:S(2)}) copy-start(bf16[64,64]{1,0:T(8,128)(2,1)} %param.20) | copy-start | bytes 24580
  98.1 46.9 %copy-start.11 = (bf16[64,512]{1,0:T(8,128)(2,1)S(1)}, bf16[64,512]{1,0:T(8,128)(2,1)}, u32[]{:S(2)}) copy-start(bf16[64,512]{1,0:T(8,128)(2,1)} %param.21) | copy-start | bytes 196612
  147.8 2.3 copy-start.14
  147.9 2.4 copy-start.15
  149.8 3.1 copy-start.20
  152.9 2.3 copy-start.22
  155.2 4.0 copy-start.18
  198.2 6.1 copy-start.5
  198.2 34.6 %all-to-all-start.2 = ((bf16[64,64,128]{2,0,1:T(8,128)(2,1)}), bf16[64,64,128]{2,0,1:T(8,128)(2,1)S(1)}, u32[]{:S(2)}, u32[]{:S(2)}) async-start(bf16[64,64,128]{2,0,1:T(8,128)(2,1)} %copy_bitcast_fusion), calls=%async_computation.2 | async-start | bytes 2097152 | tf_op jit(solution)/shard_map/all_to_all | solution.py:83
  204.0 144.5 %all-reduce.9.cloned.1.call-start = ((), (), s32[]{:S(2)}) async-start(), calls=%async_computation.4 | async-start | bytes 4718592 | tf_op jit(solution)/shard_map/psum | solution.py:101
  206.0 4.0 copy-start.17
  206.0 4.0 copy-start.19
  235.8 44.9 %copy-start.7 = (f32[64,2048]{1,0:T(8,128)S(1)}, f32[64,2048]{1,0:T(8,128)}, u32[]{:S(2)}) copy-start(f32[64,2048]{1,0:T(8,128)} %get-tuple-element.20) | copy-start | bytes 1572868
  283.6 65.0 %copy-start.2 = (f32[64,2048]{0,1:T(8,128)S(1)}, f32[64,2048]{0,1:T(8,128)}, u32[]{:S(2)}) copy-start(f32[64,2048]{0,1:T(8,128)} %scatter_custom_fusion) | copy-start | bytes 1572868
  283.7 66.2 %copy-start.3 = (f32[8192,64]{0,1:T(8,128)S(1)}, f32[8192,64]{0,1:T(8,128)}, u32[]{:S(2)}) copy-start(f32[8192,64]{0,1:T(8,128)} %copy.40) | copy-start | bytes 6291460
  283.7 331.1 %all-reduce.7.cloned.1.call-start = ((), (), s32[]{:S(2)}) async-start(), calls=%async_computation.3 | async-start | bytes 4718592 | tf_op jit(solution)/shard_map/psum | solution.py:100
  349.9 260.6 %copy-start.10 = (bf16[512,64]{0,1:T(8,128)(2,1)S(1)}, bf16[512,64]{0,1:T(8,128)(2,1)}, u32[]{:S(2)}) copy-start(bf16[512,64]{0,1:T(8,128)(2,1)} %param.18) | copy-start | bytes 196612
  617.9 3.2 copy-start.1
  (4 other events, 5.6 us)
Sparse Core Ops, SparseCore 0:
  283.8 64.7 all-reduce.8
  352.4 191.5 all-reduce.6
